TPU v7x, 256 devices: a whole 4x4x8 slice. The times are simulated.
256 devices in a mesh: row: 16 (over x, y), col: 16 (over z, core).
Axes of the slice: x: 4, y: 4, z: 8, core: 2. Of those that a mesh axis runs over, the one named last changes fastest.
Arguments:
- target: float32 [8, 16, 128, 8, 16, 128], P(None, 'row', None, None, 'col'), may hold values from -6 to 6
- panel_a: bfloat16 [2, 32, 128, 512], P(None, 'col'), may hold values from -1.1953125 to 1.1953125
- inv_factor: bfloat16 [2, 512, 512], replicated, as said below
- panel_rhs: bfloat16 [2, 512, 256], P(None, 'col'), may hold values from -6 to 6
- panel_rows: int32 [2, 32], replicated, may hold values from 0 to 127, as said below
- right_sides: float32 [8, 16, 128, 256], P(None, 'col'), may hold values from -12 to 12
Outputs:
- updated_target: float32 [8, 16, 128, 8, 16, 128], P(None, 'row', None, None, 'col')
- updated_sides: float32 [8, 16, 128, 256], P(None, 'col')
Inputs may be any that keep to these rules, and one draw needn't show every extreme that they name: `panel_rows`: each row holds 32 distinct positions in increasing order, the first 0 and the last 127. `inv_factor`: lower triangular, diagonal between 0.5 and 2.
All inputs are finite; a program needn't handle non-finite values.
Results may differ from a plain program's by a relative error of at most 0.0035.
Values may be sent and summed in bfloat16 or wider, within the bound.
A program may use at most 128 MiB of HBM per device.

v0:
```python
import jax
import jax.numpy as jnp
from jax import lax
from jax.sharding import PartitionSpec as P


def shards(target, panel_a, inv_factor, panel_rhs, panel_rows, right_sides):
    row_count = lax.axis_size("row")
    col_count = lax.axis_size("col")
    row_index = lax.axis_index("row")
    col_index = lax.axis_index("col")
    tile_rows = target.shape[2]
    row_blocks = target.shape[0]
    col_blocks = target.shape[3]
    slab_rows = tile_rows // row_count
    shard_rows = panel_rhs.shape[1]
    updated_target = target
    updated_sides = right_sides
    row_places = jnp.arange(row_blocks, dtype=jnp.int32) * row_count + row_index
    col_places = jnp.arange(col_blocks, dtype=jnp.int32) * col_count + col_index
    for which_panel in range(2):
        factor = inv_factor[which_panel]
        positions = panel_rows[which_panel]
        own_rows = lax.dynamic_slice_in_dim(
            panel_a[which_panel], row_index * slab_rows, slab_rows, 1
        )
        solved_piece = jnp.einsum(
            "axq,pq->axp", own_rows, factor, preferred_element_type=jnp.float32
        ).astype(jnp.bfloat16)
        column_tiles = lax.all_gather(solved_piece, "row", axis=1, tiled=True)
        all_tiles = lax.all_gather(column_tiles, "col", axis=0, tiled=True)
        columns = lax.dynamic_slice_in_dim(factor, col_index * shard_rows, shard_rows, 1)
        local_term = jnp.dot(columns, panel_rhs[which_panel], preferred_element_type=jnp.float32)
        partial_value = lax.psum(local_term, "col").astype(jnp.bfloat16)
        pick_rows = (positions[None, :] == row_places[:, None]).astype(jnp.bfloat16)
        pick_cols = (positions[None, :] == col_places[:, None]).astype(jnp.bfloat16)
        row_set = jnp.einsum(
            "ia,axp->ixp", pick_rows, all_tiles, preferred_element_type=jnp.float32
        ).astype(jnp.bfloat16)
        col_set = jnp.einsum(
            "ka,axp->kxp", pick_cols, all_tiles, preferred_element_type=jnp.float32
        ).astype(jnp.bfloat16)
        schur_term = jnp.einsum(
            "ixp,kyp->ixky", row_set, col_set, preferred_element_type=jnp.float32
        )
        updated_target = updated_target - schur_term[:, None, :, :, None, :]
        side_term = jnp.einsum(
            "kxp,pn->kxn", col_set, partial_value, preferred_element_type=jnp.float32
        )
        updated_sides = updated_sides - side_term[:, None]
    return (updated_target, updated_sides)


def solution(mesh):
    placed = (
        P(None, "row", None, None, "col", None),
        P(None, "col", None, None),
        P(),
        P(None, "col", None),
        P(),
        P(None, "col", None, None),
    )
    return jax.shard_map(
        shards,
        mesh=mesh,
        in_specs=placed,
        out_specs=(P(None, "row", None, None, "col", None), P(None, "col", None, None)),
        check_vma=False,
    )
```

profile of v0, /device:TPU:0, one launch (start us, length us, event | category | flops | bytes accessed | tf_op | source)
XLA Modules:
  0.0 168.0 jit_solution(11555292527745360764)
XLA Ops:
  7.2 0.0 all-gather.5.cloned.1.call-start
  7.2 1.1 fusion.73
  8.3 1.3 convolution_convert_fusion
  9.6 24.2 %all_gather.14 = bf16[2,128,512]{2,1,0:T(8,128)(2,1)} all-gather(bf16[2,8,512]{2,1,0:T(8,128)(2,1)S(1)} %convolution_convert_fusion), channel_id=1, replica_groups=mesh['row'=16,'col'=16] {'row'}, dimensions={1}, use_global_device_ids=true | all-gather | bytes 278528 | tf_op jit(solution)/shard_map/all_gather | solution.py:30
  33.8 0.0 all-gather.5.cloned.1.call-update
  33.8 0.0 all-gather.3.cloned.1.call-start
  33.9 1.3 convolution_convert_fusion.1
  35.2 25.0 %all_gather.12 = bf16[2,128,512]{2,1,0:T(8,128)(2,1)} all-gather(bf16[2,8,512]{2,1,0:T(8,128)(2,1)S(1)} %convolution_convert_fusion.1), channel_id=1, replica_groups=mesh['row'=16,'col'=16] {'row'}, dimensions={1}, use_global_device_ids=true | all-gather | bytes 278528 | tf_op jit(solution)/shard_map/all_gather | solution.py:30
  60.2 0.0 all-gather.3.cloned.1.call-update
  60.2 1.3 fusion.72
  61.5 0.3 fusion.34
  61.8 0.3 fusion.36
  62.1 69.4 %all-reduce.2 = (bf16[512,256]{1,0:T(8,128)(2,1)S(1)}, bf16[512,256]{1,0:T(8,128)(2,1)S(1)}) all-reduce(f32[512,256]{1,0:T(8,128)S(1)} %fusion.34, f32[512,256]{1,0:T(8,128)S(1)} %fusion.36), channel_id=1, replica_groups=mesh['row'=16,'col'=16] {'col'}, use_global_device_ids=true, to_apply=%region_1.0 | all-reduce | flops 262144 | bytes 1572864 | tf_op jit(solution)/shard_map/psum | solution.py:34
  131.6 0.0 all-gather.5.cloned.1.call-done
  131.6 4.5 %fusion.11 = bf16[8,128,512]{2,0,1:T(8,128)(2,1)S(1)} fusion(bf16[32,128,512]{2,1,0:T(8,128)(2,1)} %all-gather.5.cloned.1.call-done, s32[32]{0:T(128)S(1)} %get-tuple-element.12, s32[8]{0:T(128)S(1)} %fusion.68), kind=kOutput, calls=%fused_computation.13 | convolution fusion | flops 34078976 | bytes 5243040 | tf_op jit(solution)/shard_map/ka,axp->kxp/dot_general | solution.py:40
  136.2 1.7 %convolution_bitcast_fusion = f32[8,1,128,256]{3,2,0,1:T(8,128)} fusion(bf16[8,128,512]{2,0,1:T(8,128)(2,1)S(1)} %fusion.11, bf16[512,256]{1,0:T(8,128)(2,1)S(1)} %get-tuple-element.6), kind=kOutput, calls=%fused_computation.14 | convolution fusion | flops 268435456 | bytes 2359296 | tf_op jit(solution)/shard_map/kxp,pn->kxn/dot_general | solution.py:47
  137.9 4.7 %fusion.8 = bf16[8,128,512]{2,0,1:T(8,128)(2,1)S(1)} fusion(bf16[32,128,512]{2,1,0:T(8,128)(2,1)} %all-gather.3.cloned.1.call-done, s32[32]{0:T(128)S(1)} %get-tuple-element.13, s32[8]{0:T(128)S(1)} %fusion.68), kind=kOutput, calls=%fused_computation.12 | convolution fusion | flops 34078976 | bytes 5243040 | tf_op jit(solution)/shard_map/ka,axp->kxp/dot_general | solution.py:40
  142.6 2.4 %fusion.4 = bf16[8,128,512]{2,0,1:T(8,128)(2,1)S(1)} fusion(bf16[32,128,512]{2,1,0:T(8,128)(2,1)S(1)} %copy-done.1, s32[32]{0:T(128)S(1)} %get-tuple-element.13, s32[8]{0:T(128)S(1)} %fusion.69), kind=kOutput, calls=%fused_computation.6 | convolution fusion | flops 33554688 | bytes 5243040 | tf_op jit(solution)/shard_map/ia,axp->ixp/dot_general | solution.py:37
  145.0 1.6 fusion.18
  146.6 0.5 copy-done
  147.2 2.4 %fusion = bf16[8,128,512]{2,0,1:T(8,128)(2,1)S(1)} fusion(bf16[32,128,512]{2,1,0:T(8,128)(2,1)S(1)} %copy-done, s32[32]{0:T(128)S(1)} %get-tuple-element.12, s32[8]{0:T(128)S(1)} %fusion.69), kind=kOutput, calls=%fused_computation.2 | convolution fusion | flops 33554688 | bytes 5243040 | tf_op jit(solution)/shard_map/ia,axp->ixp/dot_general | solution.py:37
  149.5 2.4 %bitcast_subtract_fusion = f32[8,1,128,8,1,128]{5,2,3,0,4,1:T(8,128)S(1)} fusion(f32[8,128,8,128]{3,1,2,0:T(8,128)S(1)} %fusion.18, f32[8,1,128,8,1,128]{5,4,3,2,1,0:T(1,128)S(1)} %copy-done.2, bf16[8,128,512]{2,0,1:T(8,128)(2,1)S(1)} %fusion, bf16[8,128,512]{2,0,1:T(8,128)(2,1)S(1)} %fusion.11), kind=kOutput, calls=%fused_computation | convolution fusion | flops 1075838976 | bytes 14680064 | tf_op jit(solution)/shard_map/ixp,kyp->ixky/dot_general | solution.py:43
  151.9 6.3 %copy.26 = f32[8,1,128,8,1,128]{5,4,3,2,1,0:T(1,128)} copy(f32[8,1,128,8,1,128]{5,2,3,0,4,1:T(8,128)S(1)} %bitcast_subtract_fusion) | data formatting | bytes 8388608
  158.2 2.9 %fusion.16 = f32[8,1,128,256]{3,2,1,0:T(8,128)} fusion(f32[8,1,128,256]{3,2,0,1:T(8,128)S(1)} %copy-done.3, f32[8,1,128,256]{3,2,1,0:T(8,128)} %param.11, bf16[8,128,512]{2,0,1:T(8,128)(2,1)S(1)} %fusion.8, bf16[512,256]{1,0:T(8,128)(2,1)S(1)} %get-tuple-element.7), kind=kOutput, calls=%fused_computation.18 | convolution fusion | flops 268959744 | bytes 4456448 | tf_op jit(solution)/shard_map/kxp,pn->kxn/dot_general | solution.py:47
  (15 shorter events, 0.0 us)
Async XLA Ops:
  7.2 54.3 %copy-start.4 = (bf16[2,32,256]{2,1,0:T(8,128)(2,1)S(1)}, bf16[2,32,256]{2,1,0:T(8,128)(2,1)}, u32[]{:S(2)}) copy-start(bf16[2,32,256]{2,1,0:T(8,128)(2,1)} %param.9) | copy-start | bytes 98308
  7.2 54.9 %copy-start.5 = (s32[2,32]{1,0:T(2,128)S(1)}, s32[2,32]{1,0:T(2,128)}, u32[]{:S(2)}) copy-start(s32[2,32]{1,0:T(2,128)} %param.10) | copy-start | bytes 772
  7.2 124.4 %all-gather.5.cloned.1.call-start = ((), (), s32[]{:S(2)}) async-start(), calls=%async_computation.1 | async-start | bytes 4456448 | tf_op jit(solution)/shard_map/all_gather | solution.py:31
  33.8 104.1 %all-gather.3.cloned.1.call-start = ((), (), s32[]{:S(2)}) async-start(), calls=%async_computation | async-start | bytes 4456448 | tf_op jit(solution)/shard_map/all_gather | solution.py:31
  137.9 4.7 %copy-start.1 = (bf16[32,128,512]{2,1,0:T(8,128)(2,1)S(1)}, bf16[32,128,512]{2,1,0:T(8,128)(2,1)}, u32[]{:S(2)}) copy-start(bf16[32,128,512]{2,1,0:T(8,128)(2,1)} %all-gather.3.cloned.1.call-done) | copy-start | bytes 12582916
  145.0 2.2 %copy-start = (bf16[32,128,512]{2,1,0:T(8,128)(2,1)S(1)}, bf16[32,128,512]{2,1,0:T(8,128)(2,1)}, u32[]{:S(2)}) copy-start(bf16[32,128,512]{2,1,0:T(8,128)(2,1)} %all-gather.5.cloned.1.call-done) | copy-start | bytes 12582916
  147.2 2.4 %copy-start.2 = (f32[8,1,128,8,1,128]{5,4,3,2,1,0:T(1,128)S(1)}, f32[8,1,128,8,1,128]{5,4,3,2,1,0:T(1,128)}, u32[]{:S(2)}) copy-start(f32[8,1,128,8,1,128]{5,4,3,2,1,0:T(1,128)} %param.6) | copy-start | bytes 12582916
  151.9 6.3 %copy-start.3 = (f32[8,1,128,256]{3,2,0,1:T(8,128)S(1)}, f32[8,1,128,256]{3,2,0,1:T(8,128)}, u32[]{:S(2)}) copy-start(f32[8,1,128,256]{3,2,0,1:T(8,128)} %convolution_bitcast_fusion) | copy-start | bytes 3145732
Sparse Core Ops, SparseCore 0:
  33.9 43.4 all-gather.4
  79.3 43.1 all-gather.2
where the time goes:
time: 168 us
  blocking collectives  119 us (71%)
  matrix products  25.8 us (15%)
  between operations  14.2 us (8%)
  local copies, waits for them, and re-layouts  9.27 us (6%)
    psum x1, blocking collectives, shards(): partial_value = lax.psum(local_term, 'col').astype(jnp.bfloat16)  69.4 us
    all_gather x2, blocking collectives, shards(): column_tiles = lax.all_gather(solved_piece, 'row', axis=1, tiled=True)  49.2 us
    dot_general x2, matrix products, shards(): jnp.einsum('ka,axp->kxp', pick_cols, all_tiles, preferred_element_type=jn...  9.25 us
    unnamed x13, local copies, waits for them, and re-layouts  6.89 us
    dot_general x2, matrix products, shards(): jnp.einsum('ia,axp->ixp', pick_rows, all_tiles, preferred_element_type=jn...  4.72 us
    dot_general x2, matrix products, shards(): jnp.einsum('kxp,pn->kxn', col_set, partial_value, preferred_element_type=...  4.65 us
    dot_general x2, matrix products, shards(): jnp.einsum('ixp,kyp->ixky', row_set, col_set, preferred_element_type=jnp....  4 us
  transfers between devices with their start and end apart: 2, of which 0 were waited for; matrix products, arithmetic and copies ran while one was open for 6% of the time, Pallas kernels for 0%

commit v1 on v0

--- a/solution.py
+++ b/solution.py
@@ -31,7 +31,7 @@
         all_tiles = lax.all_gather(column_tiles, "col", axis=0, tiled=True)
         columns = lax.dynamic_slice_in_dim(factor, col_index * shard_rows, shard_rows, 1)
         local_term = jnp.dot(columns, panel_rhs[which_panel], preferred_element_type=jnp.float32)
-        partial_value = lax.psum(local_term, "col").astype(jnp.bfloat16)
+        partial_value = jnp.sum(lax.all_gather(local_term, "col"), axis=0).astype(jnp.bfloat16)
         pick_rows = (positions[None, :] == row_places[:, None]).astype(jnp.bfloat16)
         pick_cols = (positions[None, :] == col_places[:, None]).astype(jnp.bfloat16)
         row_set = jnp.einsum(

time: 168 us -> 249 us (1.48); the launches traced: 168 us -> 246 us
  waiting for transfers between devices: 0.06 us -> 138 us
  blocking collectives: 119 us -> 49.2 us
  other arithmetic: 0.01 us -> 7.89 us
    all_gather x0 -> x2, waiting for transfers between devices: none -> 90.4 us  [shards(): lax.all_gather(local_term, 'col')]
    psum x1 -> x0, blocking collectives: 69.4 us -> none  [shards(): partial_value = lax.psum(local_term, 'col').astype(jnp.bfloat16)]
    all_gather x2, waiting for transfers between devices: 0.02 us -> 47.4 us  [shards(): all_tiles = lax.all_gather(column_tiles, 'col', axis=0, tiled=True)]
    reduce_sum x0 -> x2, other arithmetic: none -> 7.88 us  [shards(): jnp.sum(lax.all_gather(local_term, 'col'), axis=0).astype(jnp.bfloat16)]
  transfers between devices with their start and end apart: 2 -> 4, of which waited for: 0 -> 4; matrix products, arithmetic and copies ran while one was open for 6% -> 14% of each run, Pallas kernels for 0% -> 0%
where the time goes in v1:
time: 249 us; the launch traced here: 246 us
  waiting for transfers between devices  138 us (55%)
  blocking collectives  49.2 us (20%)
  matrix products  27.5 us (11%)
  between operations  13.9 us (6%)
  local copies, waits for them, and re-layouts  9.55 us (4%)
  other arithmetic  7.89 us (3%)
    all_gather x2, waiting for transfers between devices, shards(): lax.all_gather(local_term, 'col')  90.4 us
    all_gather x2, blocking collectives, shards(): column_tiles = lax.all_gather(solved_piece, 'row', axis=1, tiled=True)  49.2 us
    all_gather x2, waiting for transfers between devices, shards(): all_tiles = lax.all_gather(column_tiles, 'col', axis=0, tiled=True)  47.4 us
    dot_general x2, matrix products, shards(): jnp.einsum('ka,axp->kxp', pick_cols, all_tiles, preferred_element_type=jn...  9.4 us
    reduce_sum x2, other arithmetic, shards(): jnp.sum(lax.all_gather(local_term, 'col'), axis=0).astype(jnp.bfloat16)  7.88 us
    unnamed x13, local copies, waits for them, and re-layouts  7.19 us
    dot_general x2, matrix products, shards(): jnp.einsum('ia,axp->ixp', pick_rows, all_tiles, preferred_element_type=jn...  5.71 us
  transfers between devices with their start and end apart: 4, of which 4 were waited for; matrix products, arithmetic and copies ran while one was open for 14% of the time, Pallas kernels for 0%

profile of v1, /device:TPU:0, one launch (start us, length us, event | category | flops | bytes accessed | tf_op | source)
XLA Modules:
  0.0 246.1 jit_solution(5081244638563953708)
XLA Ops:
  7.2 1.1 fusion.73
  8.3 1.3 convolution_convert_fusion
  9.6 24.2 %all_gather.26 = bf16[2,128,512]{2,1,0:T(8,128)(2,1)} all-gather(bf16[2,8,512]{2,1,0:T(8,128)(2,1)S(1)} %convolution_convert_fusion), channel_id=1, replica_groups=mesh['row'=16,'col'=16] {'row'}, dimensions={1}, use_global_device_ids=true | all-gather | bytes 278528 | tf_op jit(solution)/shard_map/all_gather | solution.py:30
  33.9 1.3 convolution_convert_fusion.1
  35.2 25.0 %all_gather.24 = bf16[2,128,512]{2,1,0:T(8,128)(2,1)} all-gather(bf16[2,8,512]{2,1,0:T(8,128)(2,1)S(1)} %convolution_convert_fusion.1), channel_id=1, replica_groups=mesh['row'=16,'col'=16] {'row'}, dimensions={1}, use_global_device_ids=true | all-gather | bytes 278528 | tf_op jit(solution)/shard_map/all_gather | solution.py:30
  60.3 1.3 fusion.72
  61.6 1.1 fusion.34
  62.8 1.1 fusion.36
  63.9 13.0 %all-gather.9.cloned.1.call-done = bf16[32,128,512]{2,1,0:T(8,128)(2,1)} async-done(((bf16[2,128,512]{2,1,0:T(8,128)(2,1)}), bf16[32,128,512]{2,1,0:T(8,128)(2,1)}) %all-gather.9.cloned.1.call-update) | async-done | bytes 4194320 | tf_op jit(solution)/shard_map/all_gather | solution.py:31
  76.9 4.7 %fusion.11 = bf16[8,128,512]{2,0,1:T(8,128)(2,1)S(1)} fusion(bf16[32,128,512]{2,1,0:T(8,128)(2,1)} %all-gather.9.cloned.1.call-done, s32[32]{0:T(128)S(1)} %get-tuple-element.10, s32[8]{0:T(128)S(1)} %fusion.68), kind=kOutput, calls=%fused_computation.13 | convolution fusion | flops 34078976 | bytes 5243040 | tf_op jit(solution)/shard_map/ka,axp->kxp/dot_general | solution.py:40
  81.6 3.3 %fusion = bf16[8,128,512]{2,0,1:T(8,128)(2,1)} fusion(bf16[32,128,512]{2,1,0:T(8,128)(2,1)S(1)} %copy-done, s32[32]{0:T(128)S(1)} %get-tuple-element.10, s32[8]{0:T(128)S(1)} %fusion.69), kind=kOutput, calls=%fused_computation.2 | convolution fusion | flops 33554688 | bytes 5243040 | tf_op jit(solution)/shard_map/ia,axp->ixp/dot_general | solution.py:37
  85.0 34.4 %all-gather.7.cloned.1.call-done = bf16[32,128,512]{2,1,0:T(8,128)(2,1)} async-done(((bf16[2,128,512]{2,1,0:T(8,128)(2,1)}), bf16[32,128,512]{2,1,0:T(8,128)(2,1)}) %all-gather.7.cloned.1.call-update) | async-done | bytes 4194320 | tf_op jit(solution)/shard_map/all_gather | solution.py:31
  119.4 4.7 %fusion.8 = bf16[8,128,512]{2,0,1:T(8,128)(2,1)S(1)} fusion(bf16[32,128,512]{2,1,0:T(8,128)(2,1)} %all-gather.7.cloned.1.call-done, s32[32]{0:T(128)S(1)} %get-tuple-element.11, s32[8]{0:T(128)S(1)} %fusion.68), kind=kOutput, calls=%fused_computation.12 | convolution fusion | flops 34078976 | bytes 5243040 | tf_op jit(solution)/shard_map/ka,axp->kxp/dot_general | solution.py:40
  124.1 2.4 fusion.4
  126.5 1.7 fusion.18
  128.2 0.8 copy-done.3
  129.0 2.3 bitcast_subtract_fusion
  131.3 6.3 %copy.26 = f32[8,1,128,8,1,128]{5,4,3,2,1,0:T(1,128)} copy(f32[8,1,128,8,1,128]{5,2,3,0,4,1:T(8,128)S(1)} %bitcast_subtract_fusion) | data formatting | bytes 8388608
  137.6 38.1 %all-gather.13.cloned.1.call-done = f32[8192,256]{1,0:T(8,128)} async-done(((f32[512,256]{1,0:T(8,128)}), f32[8192,256]{1,0:T(8,128)}) %all-gather.13.cloned.1.call-update) | async-done | bytes 8388624 | tf_op jit(solution)/shard_map/all_gather | solution.py:34
  175.7 3.9 %reduce_sum.19 = bf16[512,256]{1,0:T(8,128)(2,1)S(1)} reduce(f32[16,512,256]{2,1,0:T(8,128)} %bitcast.86, f32[]{:T(128)} %constant.24.clone.1), dimensions={0}, to_apply=%region_1.0 | reduce | flops 1966080 | bytes 8650756 | tf_op jit(solution)/shard_map/reduce_sum | solution.py:34
  179.7 52.2 %all-gather.11.cloned.1.call-done = f32[8192,256]{1,0:T(8,128)} async-done(((f32[512,256]{1,0:T(8,128)}), f32[8192,256]{1,0:T(8,128)}) %all-gather.11.cloned.1.call-update) | async-done | bytes 8388624 | tf_op jit(solution)/shard_map/all_gather | solution.py:34
  231.9 3.9 %reduce_sum.18 = bf16[512,256]{1,0:T(8,128)(2,1)S(1)} reduce(f32[16,512,256]{2,1,0:T(8,128)} %bitcast.87, f32[]{:T(128)} %constant.24.clone.1), dimensions={0}, to_apply=%region_0.0 | reduce | flops 1966080 | bytes 8650756 | tf_op jit(solution)/shard_map/reduce_sum | solution.py:34
  235.9 0.7 convolution_bitcast_fusion
  236.6 2.9 %fusion.16 = f32[8,1,128,256]{3,2,1,0:T(8,128)} fusion(f32[8,1,128,256]{3,2,0,1:T(8,128)S(1)} %convolution_bitcast_fusion, f32[8,1,128,256]{3,2,1,0:T(8,128)} %param.11, bf16[8,128,512]{2,0,1:T(8,128)(2,1)S(1)} %fusion.8, bf16[512,256]{1,0:T(8,128)(2,1)S(1)} %reduce_sum.18), kind=kOutput, calls=%fused_computation.18 | convolution fusion | flops 268959744 | bytes 4456448 | tf_op jit(solution)/shard_map/kxp,pn->kxn/dot_general | solution.py:47
  (22 shorter events, 0.3 us)
Async XLA Ops:
  7.2 54.4 %copy-start.4 = (bf16[2,32,256]{2,1,0:T(8,128)(2,1)S(1)}, bf16[2,32,256]{2,1,0:T(8,128)(2,1)}, u32[]{:S(2)}) copy-start(bf16[2,32,256]{2,1,0:T(8,128)(2,1)} %param.9) | copy-start | bytes 98308
  7.2 56.7 %copy-start.5 = (s32[2,32]{1,0:T(2,128)S(1)}, s32[2,32]{1,0:T(2,128)}, u32[]{:S(2)}) copy-start(s32[2,32]{1,0:T(2,128)} %param.10) | copy-start | bytes 772
  7.2 69.7 %all-gather.9.cloned.1.call-start = ((), (), s32[]{:S(2)}) async-start(), calls=%async_computation.1 | async-start | bytes 4456448 | tf_op jit(solution)/shard_map/all_gather | solution.py:31
  33.8 85.6 %all-gather.7.cloned.1.call-start = ((), (), s32[]{:S(2)}) async-start(), calls=%async_computation | async-start | bytes 4456448 | tf_op jit(solution)/shard_map/all_gather | solution.py:31
  60.2 115.5 %all-gather.13.cloned.1.call-start = ((), (), s32[]{:S(2)}) async-start(), calls=%async_computation.3 | async-start | bytes 8912896 | tf_op jit(solution)/shard_map/all_gather | solution.py:34
  62.7 169.2 %all-gather.11.cloned.1.call-start = ((), (), s32[]{:S(2)}) async-start(), calls=%async_computation.2 | async-start | bytes 8912896 | tf_op jit(solution)/shard_map/all_gather | solution.py:34
  76.9 4.7 %copy-start = (bf16[32,128,512]{2,1,0:T(8,128)(2,1)S(1)}, bf16[32,128,512]{2,1,0:T(8,128)(2,1)}, u32[]{:S(2)}) copy-start(bf16[32,128,512]{2,1,0:T(8,128)(2,1)} %all-gather.9.cloned.1.call-done) | copy-start | bytes 12582916
  119.4 4.7 %copy-start.1 = (bf16[32,128,512]{2,1,0:T(8,128)(2,1)S(1)}, bf16[32,128,512]{2,1,0:T(8,128)(2,1)}, u32[]{:S(2)}) copy-start(bf16[32,128,512]{2,1,0:T(8,128)(2,1)} %all-gather.7.cloned.1.call-done) | copy-start | bytes 12582916
  126.5 1.7 copy-start.2
  126.5 2.5 %copy-start.3 = (f32[8,1,128,8,1,128]{5,4,3,2,1,0:T(1,128)S(1)}, f32[8,1,128,8,1,128]{5,4,3,2,1,0:T(1,128)}, u32[]{:S(2)}) copy-start(f32[8,1,128,8,1,128]{5,4,3,2,1,0:T(1,128)} %param.6) | copy-start | bytes 12582916
Sparse Core Ops, SparseCore 0:
  33.9 42.9 all-gather.8
  78.7 40.5 all-gather.6
  121.2 54.4 all-gather.12
  177.4 54.4 all-gather.10
